TPU v7x, 256 devices: a whole 4x4x8 slice. The times are simulated.
256 devices in a mesh: sub: 16 (over z, core), dom: 16 (over y, x).
Axes of the slice: x: 4, y: 4, z: 8, core: 2. Of those that a mesh axis runs over, the one named last changes fastest.
Arguments:
- start_vectors: float32 [16, 3, 64, 16, 16, 128], P('sub', None, None, 'dom'), may hold values from -6 to 6
- face_x: float32 [16, 16, 16, 128], P('sub', 'dom'), may hold values from 0.1 to 10
- face_y: float32 [16, 16, 16, 128], P('sub', 'dom'), may hold values from 0.1 to 10
- face_z: float32 [16, 16, 16, 128], P('sub', 'dom'), may hold values from 0.1 to 10
- masses: float32 [16, 16, 16, 128], P('sub', 'dom'), may hold values from 0.5 to 2
- active: int32 [16], P('sub'), may hold values from 8 to 16, as said below
Outputs:
- deflation: bfloat16 [16, 3, 64, 16, 16, 128], P('sub', None, None, 'dom')
- coarse_diag: float32 [16, 64, 64], P('sub')
- coarse_off: float32 [16, 64, 64], P('sub')
Inputs may be any that keep to these rules, and one draw needn't show every extreme that they name: `active`: some subdomain has all 16 planes.
All inputs are finite; a program needn't handle non-finite values.
Results may differ from a plain program's by a relative error of at most 0.001.
Values sent between devices are 32-bit elements; how exact they have to be, the bound alone decides.
No kernel may reach another device: no remote copies, remote signals or barrier semaphores. Data moves between devices by JAX's collectives and lax.ppermute only.
A program may use at most 64 MiB of HBM per device.

v0:
```python
import jax
import jax.numpy as jnp
from jax import lax
from jax.sharding import PartitionSpec as P

OV = 4
STEPS = 2


def from_behind(value, axis, steps):
    count = lax.axis_size(axis)
    leading, last = (max(0, -steps), min(count, count - steps))
    return lax.ppermute(value, axis, [(source, source + steps) for source in range(leading, last)])


def with_halo(cells, sides, width):
    for axis, dim in sides:
        count = lax.axis_size(axis)
        ends = count - 1
        head = lax.slice_in_dim(cells, 0, width, axis=dim)
        tail = lax.slice_in_dim(cells, cells.shape[dim] - width, cells.shape[dim], axis=dim)
        cells = jnp.concatenate(
            [
                lax.ppermute(tail, axis, [(i, (i + 1) % count) for i in range(ends)]),
                cells,
                lax.ppermute(head, axis, [((i + 1) % count, i) for i in range(ends)]),
            ],
            axis=dim,
        )
    return cells


def gram_of(left, right):
    return jnp.einsum("ckyxz,clyxz->kl", left, right, precision=lax.Precision.HIGHEST)


def mix_cols(values, matrix):
    return jnp.einsum("ckyxz,kl->clyxz", values, matrix, precision=lax.Precision.HIGHEST)


def inverse_factor(gram_b):
    factor = jnp.linalg.cholesky(gram_b)
    identity = jnp.eye(gram_b.shape[0], dtype=jnp.float32)
    return lax.linalg.triangular_solve(factor, identity, left_side=True, lower=True)


def face_terms(values, weights, along):
    length = values.shape[along]
    head_part = lax.slice_in_dim(values, 0, length - 1, axis=along)
    tail_part = lax.slice_in_dim(values, 1, length, axis=along)
    fluxes = lax.slice_in_dim(weights, 0, length - 1, axis=along - 2)[None, None] * (
        head_part - tail_part
    )
    pad_after = [(0, 0)] * 5
    pad_after[along] = (0, 1)
    pad_before = [(0, 0)] * 5
    pad_before[along] = (1, 0)
    return jnp.pad(fluxes, pad_after) - jnp.pad(fluxes, pad_before)


def lower_faces(weights, along):
    length = weights.shape[along]
    widths = [(0, 0)] * 3
    widths[along] = (1, 0)
    return jnp.pad(lax.slice_in_dim(weights, 0, length - 1, axis=along), widths)


def on_device(start_vectors, face_x, face_y, face_z, masses, active):
    start = start_vectors[0]
    own_x = face_x[0]
    own_y = face_y[0]
    own_z = face_z[0]
    own_mass = masses[0]
    active_now = active[0]
    rows_local = own_y.shape[0]
    planes_all = own_y.shape[1]
    depth_all = own_y.shape[2]
    rows_total = rows_local * lax.axis_size("dom")
    row_index = lax.axis_index("dom") * rows_local + jnp.arange(rows_local, dtype=jnp.int32)
    plane_index = jnp.arange(planes_all, dtype=jnp.int32)
    depth_index = jnp.arange(depth_all, dtype=jnp.int32)
    inside = (plane_index < active_now)[None, :, None]
    keep_x = (plane_index + 1 < active_now)[None, :, None]
    keep_y = inside & (row_index + 1 < rows_total)[:, None, None]
    keep_z = inside & (depth_index + 1 < depth_all)[None, None, :]
    live_x = own_x * keep_x.astype(jnp.float32)
    live_y = own_y * keep_y.astype(jnp.float32)
    live_z = own_z * keep_z.astype(jnp.float32)
    below_row = from_behind(live_y, "dom", 1)
    lower_y = jnp.concatenate([below_row, live_y[:-1]], axis=0)
    diagonal = (
        live_x
        + lower_faces(live_x, 1)
        + live_y
        + lower_y
        + live_z
        + lower_faces(live_z, 2)
        + own_mass
    )
    unity = jnp.clip(
        jnp.minimum(plane_index + 1, active_now - plane_index).astype(jnp.float32) / (OV + 1),
        0.0,
        1.0,
    )[None, :, None]
    b_weight = (own_mass * unity * unity)[None, None]

    def operate(values):
        padded = with_halo(values, (("dom", 2),), 1)
        result = live_y[None, None] * (values - padded[:, :, 2:]) + lower_y[None, None] * (
            values - padded[:, :, :-2]
        )
        return result + face_terms(values, live_x, 3) + face_terms(values, live_z, 4)

    vectors = start * inside.astype(jnp.float32)[None, None]

    def normalize(values):
        gram_b = lax.psum(gram_of(values, b_weight * values), "dom")
        return mix_cols(values, inverse_factor(gram_b).T)

    for repeat in range(STEPS):
        ortho = normalize(vectors)
        image = operate(ortho)
        rayleigh = lax.psum(gram_of(ortho, image), "dom")
        residual = image - mix_cols(b_weight * ortho, rayleigh)
        vectors = ortho - 0.5 * residual / diagonal[None, None]
    deflate = unity[None, None] * normalize(vectors)
    image = operate(deflate)
    planes = lax.dynamic_slice_in_dim(image, active_now - OV, OV, axis=3)
    neighbour = from_behind(planes, "sub", 1)
    coarse_diag, coarse_off = lax.psum(
        (gram_of(deflate, image), gram_of(deflate[:, :, :, :OV], neighbour)), "dom"
    )
    return (deflate.astype(jnp.bfloat16)[None], coarse_diag[None], coarse_off[None])


def solution(mesh):
    placed = (
        P("sub", None, None, "dom", None, None),
        P("sub", "dom", None, None),
        P("sub", "dom", None, None),
        P("sub", "dom", None, None),
        P("sub", "dom", None, None),
        P("sub"),
    )
    return jax.shard_map(
        on_device,
        mesh=mesh,
        in_specs=placed,
        out_specs=(
            P("sub", None, None, "dom", None, None),
            P("sub", None, None),
            P("sub", None, None),
        ),
        check_vma=False,
    )
```

profile of v0, /device:TPU:128, one launch (start us, length us, event | category | flops | bytes accessed | tf_op | source)
XLA Modules:
  0.0 587.5 jit_solution(13905922017482201523)
XLA Ops:
  4.3 2.2 fusion.50
  6.5 74.6 %psum.49 = f32[64,64]{0,1:T(8,128)S(1)} all-reduce(f32[64,64]{0,1:T(8,128)S(1)} %fusion.50), channel_id=1, replica_groups=mesh['sub'=16,'dom'=16] {'dom'}, use_global_device_ids=true, to_apply=%region_0.1 | all-reduce | flops 4096 | bytes 32768 | tf_op jit(solution)/shard_map/psum | solution.py:117
  81.2 5.8 cholesky.59
  88.4 4.9 custom-call.7
  96.7 5.7 collective-permute-start.2
  104.8 16.0 %collective-permute-done.1 = f32[1,16,128]{2,1,0:T(8,128)S(1)} collective-permute-done((f32[1,16,128]{2,1,0:T(8,128)S(1)}, f32[1,16,128]{2,1,0:T(8,128)S(1)}, u32[]{:S(2)}, u32[]{:S(2)}) %collective-permute-start.1) | collective-permute-done | bytes 8224 | tf_op jit(solution)/shard_map/ppermute | solution.py:13
  120.9 4.1 fusion.65
  125.0 71.9 %psum.50 = f32[64,64]{0,1:T(8,128)S(1)} all-reduce(f32[64,64]{0,1:T(8,128)S(1)} %fusion.65), channel_id=1, replica_groups=mesh['sub'=16,'dom'=16] {'dom'}, use_global_device_ids=true, to_apply=%region_3.6 | all-reduce | flops 4096 | bytes 32768 | tf_op jit(solution)/shard_map/psum | solution.py:123
  196.9 6.0 %fusion.12 = f32[3,64,1,16,128]{4,1,3,0,2:T(8,128)S(1)} fusion(f32[16,128]{1,0:T(8,128)S(1)} %fusion.103, f32[16,128]{1,0:T(8,128)S(1)} %fusion.104, f32[64,64]{0,1:T(8,128)S(1)} %psum.50, f32[64,3,16,128]{3,0,2,1:T(8,128)S(1)} %fusion.32, f32[3,64,1,16,127]{4,1,3,0,2:T(8,128)} %copy-done.1, f32[3,64,1,15,128]{4,1,3,0,2:T(8,128)} %copy-done.3, ...), kind=kOutput, calls=%fused_computation.17 | convolution fusion | flops 307494912 | bytes 9375744 | tf_op jit(solution)/shard_map/ckyxz,kl->clyxz/dot_general | solution.py:38
  204.4 69.5 %psum.51 = f32[64,64]{0,1:T(8,128)S(1)} all-reduce(f32[64,64]{0,1:T(8,128)S(1)} %fusion.55), channel_id=1, replica_groups=mesh['sub'=16,'dom'=16] {'dom'}, use_global_device_ids=true, to_apply=%region_4.7 | all-reduce | flops 4096 | bytes 32768 | tf_op jit(solution)/shard_map/psum | solution.py:117
  274.0 5.8 cholesky.70
  281.2 4.9 custom-call.8
  289.2 4.6 collective-permute-start.4
  294.5 15.8 %collective-permute-done.3 = f32[3,64,1,16,128]{4,1,3,0,2:T(8,128)S(1)} collective-permute-done((f32[3,64,1,16,128]{4,1,3,0,2:T(8,128)S(1)}, f32[3,64,1,16,128]{4,1,3,0,2:T(8,128)S(1)}, u32[]{:S(2)}, u32[]{:S(2)}) %collective-permute-start.3) | collective-permute-done | bytes 1572896 | tf_op jit(solution)/shard_map/ppermute | solution.py:26
  315.1 71.9 %psum.52 = f32[64,64]{0,1:T(8,128)S(1)} all-reduce(f32[64,64]{0,1:T(8,128)S(1)} %fusion.70), channel_id=1, replica_groups=mesh['sub'=16,'dom'=16] {'dom'}, use_global_device_ids=true, to_apply=%region_5.8 | all-reduce | flops 4096 | bytes 32768 | tf_op jit(solution)/shard_map/psum | solution.py:123
  387.0 5.8 fusion.7
  394.3 69.5 %psum.53 = f32[64,64]{0,1:T(8,128)S(1)} all-reduce(f32[64,64]{0,1:T(8,128)S(1)} %fusion.60), channel_id=1, replica_groups=mesh['sub'=16,'dom'=16] {'dom'}, use_global_device_ids=true, to_apply=%region_6.9 | all-reduce | flops 4096 | bytes 32768 | tf_op jit(solution)/shard_map/psum | solution.py:117
  463.9 5.8 cholesky.81
  471.1 4.9 custom-call.9
  479.1 5.7 collective-permute-start.6
  485.4 14.6 %collective-permute-done.5 = f32[3,64,1,16,128]{4,1,3,0,2:T(8,128)S(1)} collective-permute-done((f32[3,64,1,16,128]{4,1,3,0,2:T(8,128)S(1)}, f32[3,64,1,16,128]{4,1,3,0,2:T(8,128)S(1)}, u32[]{:S(2)}, u32[]{:S(2)}) %collective-permute-start.5) | collective-permute-done | bytes 1572896 | tf_op jit(solution)/shard_map/ppermute | solution.py:26
  501.5 2.5 subtract_add_fusion
  508.9 5.4 collective-permute-done.7
  514.8 72.7 %all-reduce.14 = (f32[1,64,64]{2,1,0:T(8,128)}, f32[1,64,64]{2,1,0:T(8,128)}) all-reduce(f32[1,64,64]{2,1,0:T(8,128)S(1)} %fusion.75, f32[1,64,64]{2,1,0:T(8,128)S(1)} %convolution_bitcast_fusion), channel_id=1, replica_groups=mesh['sub'=16,'dom'=16] {'dom'}, use_global_device_ids=true, to_apply=%region_7.10 | all-reduce | flops 8192 | bytes 65536 | tf_op jit(solution)/shard_map/psum | solution.py:130
  (83 shorter events, 34.8 us)
Async XLA Ops:
  2.1 1.9 copy-start
  93.5 8.9 %copy-start.8 = (f32[1,1,16,128]{3,2,1,0:T(8,128)S(1)}, f32[1,1,16,128]{3,2,1,0:T(8,128)}, u32[]{:S(2)}) copy-start(f32[1,1,16,128]{3,2,1,0:T(8,128)} %param.11) | copy-start | bytes 24580
  93.5 10.3 %copy-start.10 = (f32[1,1,16,128]{3,2,1,0:T(8,128)S(1)}, f32[1,1,16,128]{3,2,1,0:T(8,128)}, u32[]{:S(2)}) copy-start(f32[1,1,16,128]{3,2,1,0:T(8,128)} %param.12) | copy-start | bytes 24580
  93.6 10.4 %copy-start.11 = (f32[1,1,16,128]{3,2,1,0:T(8,128)S(1)}, f32[1,1,16,128]{3,2,1,0:T(8,128)}, u32[]{:S(2)}) copy-start(f32[1,1,16,128]{3,2,1,0:T(8,128)} %param.10) | copy-start | bytes 24580
  95.4 25.4 %collective-permute-start = (f32[3,64,1,16,128]{4,1,3,0,2:T(8,128)S(1)}, f32[3,64,1,16,128]{4,1,3,0,2:T(8,128)S(1)}, u32[]{:S(2)}, u32[]{:S(2)}) collective-permute-start(f32[3,64,1,16,128]{4,1,3,0,2:T(8,128)S(1)} %bitcast.253), channel_id=1, source_target_pairs={{1,0},{2,1},{3,2},{4,3},{5,4},{6,5},{7,6},{8,7},{9,8},{10,9},{11,1... | collective-permute-start | bytes 4718600 | tf_op jit(solution)/shard_map/ppermute | solution.py:26
  96.7 24.1 %collective-permute-start.2 = (f32[3,64,1,16,128]{4,1,3,0,2:T(8,128)S(1)}, f32[3,64,1,16,128]{4,1,3,0,2:T(8,128)}, u32[]{:S(2)}, u32[]{:S(2)}) collective-permute-start(f32[3,64,1,16,128]{4,1,3,0,2:T(8,128)S(1)} %bitcast.254), channel_id=1, source_target_pairs={{0,1},{1,2},{2,3},{3,4},{4,5},{5,6},{6,7},{7,8},{8,9},{9,10},{10,1... | collective-permute-start | bytes 4718600 | tf_op jit(solution)/shard_map/ppermute | solution.py:24
  102.5 18.2 %collective-permute-start.1 = (f32[1,16,128]{2,1,0:T(8,128)S(1)}, f32[1,16,128]{2,1,0:T(8,128)S(1)}, u32[]{:S(2)}, u32[]{:S(2)}) collective-permute-start(f32[1,16,128]{2,1,0:T(8,128)S(1)} %bitcast_multiply_fusion.3), channel_id=1, source_target_pairs={{0,1},{1,2},{2,3},{3,4},{4,5},{5,6},{6,7},{7,8},{8,9},{9,10},{10,1... | collective-permute-start | bytes 24584 | tf_op jit(solution)/shard_map/ppermute | solution.py:13
  104.2 16.7 %copy-start.3 = (f32[3,64,1,15,128]{4,1,3,0,2:T(8,128)}, f32[3,64,1,15,128]{4,1,3,0,2:T(8,128)S(1)}, u32[]{:S(2)}) copy-start(f32[3,64,1,15,128]{4,1,3,0,2:T(8,128)S(1)} %fusion.49) | copy-start | bytes 4423684
  104.2 16.6 %copy-start.9 = (f32[1,1,16,128]{3,2,1,0:T(8,128)S(1)}, f32[1,1,16,128]{3,2,1,0:T(8,128)}, u32[]{:S(2)}) copy-start(f32[1,1,16,128]{3,2,1,0:T(8,128)} %param.13) | copy-start | bytes 24580
  104.7 16.2 %copy-start.1 = (f32[3,64,1,16,127]{4,1,3,0,2:T(8,128)}, f32[3,64,1,16,127]{4,1,3,0,2:T(8,128)S(1)}, u32[]{:S(2)}) copy-start(f32[3,64,1,16,127]{4,1,3,0,2:T(8,128)S(1)} %fusion.2) | copy-start | bytes 4681732
  120.9 4.1 copy-start.5
  287.9 22.5 %collective-permute-start.3 = (f32[3,64,1,16,128]{4,1,3,0,2:T(8,128)S(1)}, f32[3,64,1,16,128]{4,1,3,0,2:T(8,128)S(1)}, u32[]{:S(2)}, u32[]{:S(2)}) collective-permute-start(f32[3,64,1,16,128]{4,1,3,0,2:T(8,128)S(1)} %bitcast.257), channel_id=1, source_target_pairs={{1,0},{2,1},{3,2},{4,3},{5,4},{6,5},{7,6},{8,7},{9,8},{10,9},{11,1... | collective-permute-start | bytes 4718600 | tf_op jit(solution)/shard_map/ppermute | solution.py:26
  289.2 22.7 %collective-permute-start.4 = (f32[3,64,1,16,128]{4,1,3,0,2:T(8,128)S(1)}, f32[3,64,1,16,128]{4,1,3,0,2:T(8,128)S(1)}, u32[]{:S(2)}, u32[]{:S(2)}) collective-permute-start(f32[3,64,1,16,128]{4,1,3,0,2:T(8,128)S(1)} %bitcast.258), channel_id=1, source_target_pairs={{0,1},{1,2},{2,3},{3,4},{4,5},{5,6},{6,7},{7,8},{8,9},{9,10},{10,1... | collective-permute-start | bytes 4718600 | tf_op jit(solution)/shard_map/ppermute | solution.py:24
  294.0 17.9 %copy-start.4 = (f32[3,64,1,15,128]{4,1,3,0,2:T(8,128)}, f32[3,64,1,15,128]{4,1,3,0,2:T(8,128)S(1)}, u32[]{:S(2)}) copy-start(f32[3,64,1,15,128]{4,1,3,0,2:T(8,128)S(1)} %fusion.48) | copy-start | bytes 4423684
  294.5 17.4 %copy-start.2 = (f32[3,64,1,16,127]{4,1,3,0,2:T(8,128)}, f32[3,64,1,16,127]{4,1,3,0,2:T(8,128)S(1)}, u32[]{:S(2)}) copy-start(f32[3,64,1,16,127]{4,1,3,0,2:T(8,128)S(1)} %fusion.1) | copy-start | bytes 4681732
  310.3 1.5 copy-start.6
  311.9 1.1 copy-start.7
  477.8 22.3 %collective-permute-start.5 = (f32[3,64,1,16,128]{4,1,3,0,2:T(8,128)S(1)}, f32[3,64,1,16,128]{4,1,3,0,2:T(8,128)S(1)}, u32[]{:S(2)}, u32[]{:S(2)}) collective-permute-start(f32[3,64,1,16,128]{4,1,3,0,2:T(8,128)S(1)} %bitcast.248), channel_id=1, source_target_pairs={{1,0},{2,1},{3,2},{4,3},{5,4},{6,5},{7,6},{8,7},{9,8},{10,9},{11,1... | collective-permute-start | bytes 4718600 | tf_op jit(solution)/shard_map/ppermute | solution.py:26
  479.1 22.5 %collective-permute-start.6 = (f32[3,64,1,16,128]{4,1,3,0,2:T(8,128)S(1)}, f32[3,64,1,16,128]{4,1,3,0,2:T(8,128)}, u32[]{:S(2)}, u32[]{:S(2)}) collective-permute-start(f32[3,64,1,16,128]{4,1,3,0,2:T(8,128)S(1)} %bitcast.249), channel_id=1, source_target_pairs={{0,1},{1,2},{2,3},{3,4},{4,5},{5,6},{6,7},{7,8},{8,9},{9,10},{10,1... | collective-permute-start | bytes 4718600 | tf_op jit(solution)/shard_map/ppermute | solution.py:24
  504.1 10.3 %collective-permute-start.7 = (f32[3,64,1,4,128]{4,1,3,0,2:T(8,128)S(1)}, f32[3,64,1,4,128]{4,1,3,0,2:T(8,128)S(1)}, u32[]{:S(2)}, u32[]{:S(2)}) collective-permute-start(f32[3,64,1,4,128]{4,1,3,0,2:T(8,128)S(1)} %constant_dynamic-slice_fusion), channel_id=1, source_target_pairs={{0,16},{16,32},{32,48},{48,64},{64,80},{80,96},{96,112},{112,128},... | collective-permute-start | bytes 1179656 | tf_op jit(solution)/shard_map/ppermute | solution.py:13
where the time goes:
time: 588 us
  blocking collectives  430 us (73%)
  waiting for transfers between devices  54.9 us (9%)
  other arithmetic  44.1 us (8%)
  matrix products  30.6 us (5%)
  starting transfers between devices  23.1 us (4%)
    psum x3, blocking collectives, normalize(): gram_b = lax.psum(gram_of(values, b_weight * values), 'dom')  214 us
    psum x2, blocking collectives, on_device(): rayleigh = lax.psum(gram_of(ortho, image), 'dom')  144 us
    psum x1, blocking collectives, on_device(): lax.psum((gram_of(deflate, image), gram_of(deflate[:, :, :, :OV], neighbo...  72.7 us
    ppermute x3, waiting for transfers between devices, with_halo(): lax.ppermute(head, axis, [((i + 1) % count, i) for i in range(ends)])  30.5 us
    ppermute x2, waiting for transfers between devices, from_behind(): lax.ppermute(value, axis, [(source, source + steps) for source in range(l...  21.4 us
    another operation x9, other arithmetic, inverse_factor(): factor = jnp.linalg.cholesky(gram_b)  19.6 us
    dot_general x5, matrix products, mix_cols(): jnp.einsum('ckyxz,kl->clyxz', values, matrix, precision=lax.Precision.HIG...  16.7 us
    another operation x6, other arithmetic, inverse_factor(): lax.linalg.triangular_solve(factor, identity, left_side=True, lower=True)  16.6 us
  transfers between devices with their start and end apart: 8, of which 6 were waited for; matrix products, arithmetic and copies ran while one was open for 1% of the time, Pallas kernels for 0%

commit v1 on v0

--- a/solution.py
+++ b/solution.py
@@ -120,7 +120,9 @@
     for repeat in range(STEPS):
         ortho = normalize(vectors)
         image = operate(ortho)
-        rayleigh = lax.psum(gram_of(ortho, image), "dom")
+        x = gram_of(ortho, image)
+        terms = lax.all_gather(x, "dom", axis=0, tiled=False)
+        rayleigh = terms.sum(axis=0)
         residual = image - mix_cols(b_weight * ortho, rayleigh)
         vectors = ortho - 0.5 * residual / diagonal[None, None]
     deflate = unity[None, None] * normalize(vectors)

time: 588 us -> 497 us (0.85)
  blocking collectives: 430 us -> 339 us
    psum x2 -> x0, blocking collectives: 144 us -> none  [on_device(): rayleigh = lax.psum(gram_of(ortho, image), 'dom')]
    all_gather x0 -> x2, blocking collectives: none -> 47.3 us  [on_device(): terms = lax.all_gather(x, 'dom', axis=0, tiled=False)]
where the time goes in v1:
time: 497 us; the launch traced here: 496 us
  blocking collectives  339 us (68%)
  waiting for transfers between devices  54.8 us (11%)
  other arithmetic  44.2 us (9%)
  matrix products  30.4 us (6%)
  starting transfers between devices  23.4 us (5%)
    psum x3, blocking collectives, normalize(): gram_b = lax.psum(gram_of(values, b_weight * values), 'dom')  219 us
    psum x1, blocking collectives, on_device(): lax.psum((gram_of(deflate, image), gram_of(deflate[:, :, :, :OV], neighbo...  72.7 us
    all_gather x2, blocking collectives, on_device(): terms = lax.all_gather(x, 'dom', axis=0, tiled=False)  47.3 us
    ppermute x3, waiting for transfers between devices, with_halo(): lax.ppermute(head, axis, [((i + 1) % count, i) for i in range(ends)])  30.7 us
    ppermute x2, waiting for transfers between devices, from_behind(): lax.ppermute(value, axis, [(source, source + steps) for source in range(l...  21.3 us
    another operation x9, other arithmetic, inverse_factor(): factor = jnp.linalg.cholesky(gram_b)  19.6 us
    dot_general x5, matrix products, mix_cols(): jnp.einsum('ckyxz,kl->clyxz', values, matrix, precision=lax.Precision.HIG...  17 us
    another operation x6, other arithmetic, inverse_factor(): lax.linalg.triangular_solve(factor, identity, left_side=True, lower=True)  16.6 us
  transfers between devices with their start and end apart: 8, of which 6 were waited for; matrix products, arithmetic and copies ran while one was open for 1% of the time, Pallas kernels for 0%

profile of v1, /device:TPU:128, one launch (start us, length us, event | category | flops | bytes accessed | tf_op | source)
XLA Modules:
  0.0 496.1 jit_solution(17293580408716420935)
XLA Ops:
  4.3 2.2 fusion.50
  6.5 74.6 %psum.35 = f32[64,64]{0,1:T(8,128)S(1)} all-reduce(f32[64,64]{0,1:T(8,128)S(1)} %fusion.50), channel_id=1, replica_groups=mesh['sub'=16,'dom'=16] {'dom'}, use_global_device_ids=true, to_apply=%region_0.1 | all-reduce | flops 4096 | bytes 32768 | tf_op jit(solution)/shard_map/psum | solution.py:117
  81.2 5.8 %cholesky.59 = f32[64,64]{1,0:T(8,128)S(1)} custom-call(f32[64,64]{1,0:T(8,128)S(1)} %fusion.98), custom_call_target="Cholesky" | custom-call | tf_op jit(solution)/shard_map/jit(cholesky)/cholesky | solution.py:42
  88.4 4.9 custom-call.7
  96.7 5.7 %collective-permute-start.2 = (f32[3,64,1,16,128]{4,1,3,0,2:T(8,128)S(1)}, f32[3,64,1,16,128]{4,1,3,0,2:T(8,128)}, u32[]{:S(2)}, u32[]{:S(2)}) collective-permute-start(f32[3,64,1,16,128]{4,1,3,0,2:T(8,128)S(1)} %bitcast.252), channel_id=1, source_target_pairs={{0,1},{1,2},{2,3},{3,4},{4,5},{5,6},{6,7},{7,8},{8,9},{9,10},{10,1... | collective-permute-start | bytes 4718600 | tf_op jit(solution)/shard_map/ppermute | solution.py:24
  104.8 16.1 %collective-permute-done.1 = f32[1,16,128]{2,1,0:T(8,128)S(1)} collective-permute-done((f32[1,16,128]{2,1,0:T(8,128)S(1)}, f32[1,16,128]{2,1,0:T(8,128)S(1)}, u32[]{:S(2)}, u32[]{:S(2)}) %collective-permute-start.1) | collective-permute-done | bytes 8224 | tf_op jit(solution)/shard_map/ppermute | solution.py:13
  122.1 3.5 fusion.65
  125.7 23.6 %all-gather = f32[1024,64]{1,0:T(8,128)S(1)} all-gather(f32[64,64]{1,0:T(8,128)S(1)} %fusion.65), channel_id=2, replica_groups=mesh['sub'=16,'dom'=16] {'dom'}, dimensions={0}, use_global_device_ids=true | all-gather | bytes 278528 | tf_op jit(solution)/shard_map/all_gather | solution.py:124
  149.4 6.2 %fusion.12 = f32[3,64,1,16,128]{4,1,3,0,2:T(8,128)S(1)} fusion(f32[16,128]{1,0:T(8,128)S(1)} %fusion.103, f32[16,128]{1,0:T(8,128)S(1)} %fusion.104, f32[64,64]{1,0:T(8,128)S(1)} %reduce_sum.18, f32[64,3,16,128]{3,0,2,1:T(8,128)S(1)} %fusion.32, f32[3,64,1,16,127]{4,1,3,0,2:T(8,128)} %copy-done.1, f32[3,64,1,15,128]{4,1,3,0,2:T(8,128)} %copy-done.3, ...), kind=kOutput, calls=%fused_computation.17 | convolution fusion | flops 307494912 | bytes 9375744 | tf_op jit(solution)/shard_map/ckyxz,kl->clyxz/dot_general | solution.py:38
  157.0 72.1 %psum.36 = f32[64,64]{0,1:T(8,128)S(1)} all-reduce(f32[64,64]{0,1:T(8,128)S(1)} %fusion.55), channel_id=1, replica_groups=mesh['sub'=16,'dom'=16] {'dom'}, use_global_device_ids=true, to_apply=%region_4.7 | all-reduce | flops 4096 | bytes 32768 | tf_op jit(solution)/shard_map/psum | solution.py:117
  229.2 5.8 %cholesky.70 = f32[64,64]{1,0:T(8,128)S(1)} custom-call(f32[64,64]{1,0:T(8,128)S(1)} %fusion.95), custom_call_target="Cholesky" | custom-call | tf_op jit(solution)/shard_map/jit(cholesky)/cholesky | solution.py:42
  236.3 4.9 custom-call.8
  244.3 4.6 collective-permute-start.4
  249.6 16.1 %collective-permute-done.3 = f32[3,64,1,16,128]{4,1,3,0,2:T(8,128)S(1)} collective-permute-done((f32[3,64,1,16,128]{4,1,3,0,2:T(8,128)S(1)}, f32[3,64,1,16,128]{4,1,3,0,2:T(8,128)S(1)}, u32[]{:S(2)}, u32[]{:S(2)}) %collective-permute-start.3) | collective-permute-done | bytes 1572896 | tf_op jit(solution)/shard_map/ppermute | solution.py:26
  269.3 23.6 %all-gather.1 = f32[1024,64]{1,0:T(8,128)S(1)} all-gather(f32[64,64]{1,0:T(8,128)S(1)} %fusion.70), channel_id=3, replica_groups=mesh['sub'=16,'dom'=16] {'dom'}, dimensions={0}, use_global_device_ids=true | all-gather | bytes 278528 | tf_op jit(solution)/shard_map/all_gather | solution.py:124
  293.0 6.0 %fusion.7 = f32[3,64,1,16,128]{4,1,3,0,2:T(8,128)S(1)} fusion(f32[16,128]{1,0:T(8,128)S(1)} %fusion.103, f32[16,128]{1,0:T(8,128)S(1)} %fusion.104, f32[64,64]{1,0:T(8,128)S(1)} %reduce_sum.19, f32[64,3,16,128]{3,0,2,1:T(8,128)S(1)} %fusion.26, f32[3,64,1,16,127]{4,1,3,0,2:T(8,128)} %copy-done.2, f32[3,64,1,15,128]{4,1,3,0,2:T(8,128)} %copy-done.4, ...), kind=kOutput, calls=%fused_computation.11 | convolution fusion | flops 307494912 | bytes 9375744 | tf_op jit(solution)/shard_map/ckyxz,kl->clyxz/dot_general | solution.py:38
  300.4 72.0 %psum.37 = f32[64,64]{0,1:T(8,128)S(1)} all-reduce(f32[64,64]{0,1:T(8,128)S(1)} %fusion.60), channel_id=1, replica_groups=mesh['sub'=16,'dom'=16] {'dom'}, use_global_device_ids=true, to_apply=%region_6.9 | all-reduce | flops 4096 | bytes 32768 | tf_op jit(solution)/shard_map/psum | solution.py:117
  372.5 5.8 %cholesky.81 = f32[64,64]{1,0:T(8,128)S(1)} custom-call(f32[64,64]{1,0:T(8,128)S(1)} %fusion.92), custom_call_target="Cholesky" | custom-call | tf_op jit(solution)/shard_map/jit(cholesky)/cholesky | solution.py:42
  379.7 4.9 custom-call.9
  387.7 5.7 %collective-permute-start.6 = (f32[3,64,1,16,128]{4,1,3,0,2:T(8,128)S(1)}, f32[3,64,1,16,128]{4,1,3,0,2:T(8,128)}, u32[]{:S(2)}, u32[]{:S(2)}) collective-permute-start(f32[3,64,1,16,128]{4,1,3,0,2:T(8,128)S(1)} %bitcast.247), channel_id=1, source_target_pairs={{0,1},{1,2},{2,3},{3,4},{4,5},{5,6},{6,7},{7,8},{8,9},{9,10},{10,1... | collective-permute-start | bytes 4718600 | tf_op jit(solution)/shard_map/ppermute | solution.py:24
  394.0 14.6 %collective-permute-done.5 = f32[3,64,1,16,128]{4,1,3,0,2:T(8,128)S(1)} collective-permute-done((f32[3,64,1,16,128]{4,1,3,0,2:T(8,128)S(1)}, f32[3,64,1,16,128]{4,1,3,0,2:T(8,128)S(1)}, u32[]{:S(2)}, u32[]{:S(2)}) %collective-permute-start.5) | collective-permute-done | bytes 1572896 | tf_op jit(solution)/shard_map/ppermute | solution.py:26
  410.1 2.5 subtract_add_fusion
  417.8 5.2 %collective-permute-done.7 = f32[3,64,1,4,128]{4,1,3,0,2:T(8,128)S(1)} collective-permute-done((f32[3,64,1,4,128]{4,1,3,0,2:T(8,128)S(1)}, f32[3,64,1,4,128]{4,1,3,0,2:T(8,128)S(1)}, u32[]{:S(2)}, u32[]{:S(2)}) %collective-permute-start.7) | collective-permute-done | bytes 393248 | tf_op jit(solution)/shard_map/ppermute | solution.py:13
  423.4 72.7 %all-reduce.14 = (f32[1,64,64]{2,1,0:T(8,128)}, f32[1,64,64]{2,1,0:T(8,128)}) all-reduce(f32[1,64,64]{2,1,0:T(8,128)S(1)} %fusion.75, f32[1,64,64]{2,1,0:T(8,128)S(1)} %convolution_bitcast_fusion), channel_id=1, replica_groups=mesh['sub'=16,'dom'=16] {'dom'}, use_global_device_ids=true, to_apply=%region_7.10 | all-reduce | flops 8192 | bytes 65536 | tf_op jit(solution)/shard_map/psum | solution.py:132
  (85 shorter events, 35.1 us)
Async XLA Ops:
  2.1 1.9 copy-start
  93.5 8.9 %copy-start.8 = (f32[1,1,16,128]{3,2,1,0:T(8,128)S(1)}, f32[1,1,16,128]{3,2,1,0:T(8,128)}, u32[]{:S(2)}) copy-start(f32[1,1,16,128]{3,2,1,0:T(8,128)} %param.11) | copy-start | bytes 24580
  93.5 10.3 %copy-start.10 = (f32[1,1,16,128]{3,2,1,0:T(8,128)S(1)}, f32[1,1,16,128]{3,2,1,0:T(8,128)}, u32[]{:S(2)}) copy-start(f32[1,1,16,128]{3,2,1,0:T(8,128)} %param.12) | copy-start | bytes 24580
  93.6 10.4 %copy-start.11 = (f32[1,1,16,128]{3,2,1,0:T(8,128)S(1)}, f32[1,1,16,128]{3,2,1,0:T(8,128)}, u32[]{:S(2)}) copy-start(f32[1,1,16,128]{3,2,1,0:T(8,128)} %param.10) | copy-start | bytes 24580
  95.4 25.5 %collective-permute-start = (f32[3,64,1,16,128]{4,1,3,0,2:T(8,128)S(1)}, f32[3,64,1,16,128]{4,1,3,0,2:T(8,128)S(1)}, u32[]{:S(2)}, u32[]{:S(2)}) collective-permute-start(f32[3,64,1,16,128]{4,1,3,0,2:T(8,128)S(1)} %bitcast.251), channel_id=1, source_target_pairs={{1,0},{2,1},{3,2},{4,3},{5,4},{6,5},{7,6},{8,7},{9,8},{10,9},{11,1... | collective-permute-start | bytes 4718600 | tf_op jit(solution)/shard_map/ppermute | solution.py:26
  96.7 24.3 %collective-permute-start.2 = (f32[3,64,1,16,128]{4,1,3,0,2:T(8,128)S(1)}, f32[3,64,1,16,128]{4,1,3,0,2:T(8,128)}, u32[]{:S(2)}, u32[]{:S(2)}) collective-permute-start(f32[3,64,1,16,128]{4,1,3,0,2:T(8,128)S(1)} %bitcast.252), channel_id=1, source_target_pairs={{0,1},{1,2},{2,3},{3,4},{4,5},{5,6},{6,7},{7,8},{8,9},{9,10},{10,1... | collective-permute-start | bytes 4718600 | tf_op jit(solution)/shard_map/ppermute | solution.py:24
  102.5 18.4 %collective-permute-start.1 = (f32[1,16,128]{2,1,0:T(8,128)S(1)}, f32[1,16,128]{2,1,0:T(8,128)S(1)}, u32[]{:S(2)}, u32[]{:S(2)}) collective-permute-start(f32[1,16,128]{2,1,0:T(8,128)S(1)} %bitcast_multiply_fusion.3), channel_id=1, source_target_pairs={{0,1},{1,2},{2,3},{3,4},{4,5},{5,6},{6,7},{7,8},{8,9},{9,10},{10,1... | collective-permute-start | bytes 24584 | tf_op jit(solution)/shard_map/ppermute | solution.py:13
  104.2 16.8 %copy-start.3 = (f32[3,64,1,15,128]{4,1,3,0,2:T(8,128)}, f32[3,64,1,15,128]{4,1,3,0,2:T(8,128)S(1)}, u32[]{:S(2)}) copy-start(f32[3,64,1,15,128]{4,1,3,0,2:T(8,128)S(1)} %fusion.49) | copy-start | bytes 4423684
  104.2 16.7 %copy-start.9 = (f32[1,1,16,128]{3,2,1,0:T(8,128)S(1)}, f32[1,1,16,128]{3,2,1,0:T(8,128)}, u32[]{:S(2)}) copy-start(f32[1,1,16,128]{3,2,1,0:T(8,128)} %param.13) | copy-start | bytes 24580
  104.7 21.0 %copy-start.1 = (f32[3,64,1,16,127]{4,1,3,0,2:T(8,128)}, f32[3,64,1,16,127]{4,1,3,0,2:T(8,128)S(1)}, u32[]{:S(2)}) copy-start(f32[3,64,1,16,127]{4,1,3,0,2:T(8,128)S(1)} %fusion.2) | copy-start | bytes 4681732
  121.0 1.1 copy-start.5
  243.0 22.7 %collective-permute-start.3 = (f32[3,64,1,16,128]{4,1,3,0,2:T(8,128)S(1)}, f32[3,64,1,16,128]{4,1,3,0,2:T(8,128)S(1)}, u32[]{:S(2)}, u32[]{:S(2)}) collective-permute-start(f32[3,64,1,16,128]{4,1,3,0,2:T(8,128)S(1)} %bitcast.255), channel_id=1, source_target_pairs={{1,0},{2,1},{3,2},{4,3},{5,4},{6,5},{7,6},{8,7},{9,8},{10,9},{11,1... | collective-permute-start | bytes 4718600 | tf_op jit(solution)/shard_map/ppermute | solution.py:26
  244.3 22.7 %collective-permute-start.4 = (f32[3,64,1,16,128]{4,1,3,0,2:T(8,128)S(1)}, f32[3,64,1,16,128]{4,1,3,0,2:T(8,128)S(1)}, u32[]{:S(2)}, u32[]{:S(2)}) collective-permute-start(f32[3,64,1,16,128]{4,1,3,0,2:T(8,128)S(1)} %bitcast.256), channel_id=1, source_target_pairs={{0,1},{1,2},{2,3},{3,4},{4,5},{5,6},{6,7},{7,8},{8,9},{9,10},{10,1... | collective-permute-start | bytes 4718600 | tf_op jit(solution)/shard_map/ppermute | solution.py:24
  249.1 17.9 %copy-start.4 = (f32[3,64,1,15,128]{4,1,3,0,2:T(8,128)}, f32[3,64,1,15,128]{4,1,3,0,2:T(8,128)S(1)}, u32[]{:S(2)}) copy-start(f32[3,64,1,15,128]{4,1,3,0,2:T(8,128)S(1)} %fusion.48) | copy-start | bytes 4423684
  249.6 19.6 %copy-start.2 = (f32[3,64,1,16,127]{4,1,3,0,2:T(8,128)}, f32[3,64,1,16,127]{4,1,3,0,2:T(8,128)S(1)}, u32[]{:S(2)}) copy-start(f32[3,64,1,16,127]{4,1,3,0,2:T(8,128)S(1)} %fusion.1) | copy-start | bytes 4681732
  265.7 3.5 copy-start.6
  267.1 2.2 copy-start.7
  386.4 22.3 %collective-permute-start.5 = (f32[3,64,1,16,128]{4,1,3,0,2:T(8,128)S(1)}, f32[3,64,1,16,128]{4,1,3,0,2:T(8,128)S(1)}, u32[]{:S(2)}, u32[]{:S(2)}) collective-permute-start(f32[3,64,1,16,128]{4,1,3,0,2:T(8,128)S(1)} %bitcast.246), channel_id=1, source_target_pairs={{1,0},{2,1},{3,2},{4,3},{5,4},{6,5},{7,6},{8,7},{9,8},{10,9},{11,1... | collective-permute-start | bytes 4718600 | tf_op jit(solution)/shard_map/ppermute | solution.py:26
  387.7 22.5 %collective-permute-start.6 = (f32[3,64,1,16,128]{4,1,3,0,2:T(8,128)S(1)}, f32[3,64,1,16,128]{4,1,3,0,2:T(8,128)}, u32[]{:S(2)}, u32[]{:S(2)}) collective-permute-start(f32[3,64,1,16,128]{4,1,3,0,2:T(8,128)S(1)} %bitcast.247), channel_id=1, source_target_pairs={{0,1},{1,2},{2,3},{3,4},{4,5},{5,6},{6,7},{7,8},{8,9},{9,10},{10,1... | collective-permute-start | bytes 4718600 | tf_op jit(solution)/shard_map/ppermute | solution.py:24
  412.7 10.3 %collective-permute-start.7 = (f32[3,64,1,4,128]{4,1,3,0,2:T(8,128)S(1)}, f32[3,64,1,4,128]{4,1,3,0,2:T(8,128)S(1)}, u32[]{:S(2)}, u32[]{:S(2)}) collective-permute-start(f32[3,64,1,4,128]{4,1,3,0,2:T(8,128)S(1)} %constant_dynamic-slice_fusion), channel_id=1, source_target_pairs={{0,16},{16,32},{32,48},{48,64},{64,80},{80,96},{96,112},{112,128},... | collective-permute-start | bytes 1179656 | tf_op jit(solution)/shard_map/ppermute | solution.py:13
